TPU v7x, 256 devices: a whole 4x4x8 slice. The times are simulated.
256 devices in a mesh: row: 8 (over y, x_lo), col: 32 (over z, x_hi, core).
Axes of the slice: x: 4 (x_hi: 2, x_lo: 2; x = x_hi * 2 + x_lo), y: 4, z: 8, core: 2. Of those that a mesh axis runs over, the one named last changes fastest.
Arguments:
- observed: float32 [16, 1024, 4096], P(None, 'row', 'col'), may hold values from 0.2 to 3
- estimate: float32 [16, 1024, 4096], P(None, 'row', 'col'), may hold values from 0.5 to 2
- psf_bank: float32 [1024, 16, 2, 4, 33], P(('row', 'col')), may hold values from 0.05 to 1
- zone_ids: int32 [8, 32, 16, 2], P('row', 'col'), may hold values from 0 to 127, all different within a row
- mix_weights: float32 [8, 32, 16, 2], P('row', 'col'), may hold values from 0.2 to 1
- illumination: float32 [16, 128, 32], P(None, 'row', 'col'), may hold values from 0.3 to 3
Outputs:
- restored: float32 [16, 1024, 4096], P(None, 'row', 'col')
Inputs may be any that keep to these rules, and one draw needn't show every extreme that they name: `zone_ids`: at each depth a tile names 2 different zones.
All inputs are finite; a program needn't handle non-finite values.
Results may differ from a plain program's by a relative error of at most 0.001.
Values may be sent and summed in bfloat16 or wider, within the bound.
A program may use at most 192 MiB of HBM per device.

v0:
```python
import functools

import jax
import jax.numpy as jnp
import numpy as np
from jax import lax
from jax.experimental import pallas as pl
from jax.experimental.pallas import tpu as pltpu
from jax.sharding import PartitionSpec as P

MESH = pl.DeviceIdType.MESH
BF = jnp.bfloat16
F32 = jnp.float32
TAPS = 33
HALF = 16
GZ = 4
NT = (((1,), (1,)), ((), ()))


def mm(a, b):
    return jnp.dot(a, b, preferred_element_type=F32)


def mm_nt(a, b):
    return lax.dot_general(a, b, NT, preferred_element_type=F32)


def spread_table():
    w = np.zeros((128, 6 * 128), np.float32)
    for a in range(TAPS):
        plus, minus = (a - HALF) % 128, (HALF - a) % 128
        for lane in (a, TAPS + a):
            w[lane, minus] = 1.0
            w[lane, 128 + plus] = 1.0
            w[lane, 512:640] = 1.0
        w[2 * TAPS + a, 256 + plus] = 1.0
        w[2 * TAPS + a, 384 + minus] = 1.0
    w[3 * TAPS : 3 * TAPS + 3, 640:768] = 1.0
    return w.astype(BF)


def moves_table():
    eye = np.eye(128, dtype=np.float32)
    ends = np.concatenate([eye[:16], eye[112:]], 0)
    place = np.zeros((GZ, 128, 128), np.float32)
    sel_r = np.zeros((GZ * 16, 128), np.float32)
    sel_l = np.zeros((GZ * 16, 128), np.float32)
    for zz in range(GZ):
        for i in range(16):
            place[zz, i, zz * 32 + i] = 1.0
            place[zz, 112 + i, zz * 32 + 16 + i] = 1.0
            sel_r[zz * 16 + i, zz * 32 + i] = 1.0
            sel_l[zz * 16 + i, zz * 32 + 16 + i] = 1.0
    return np.concatenate([eye, ends, place.reshape(-1, 128), sel_r, sel_l], 0).astype(BF)


def smoothing_table(length, n_row, rows):
    stiff = float(length * length) / 16.0
    d = np.diff(np.eye(length), axis=0)
    inv = np.linalg.inv(np.eye(length) + stiff * d.T @ d)
    rep = np.repeat(inv, rows * n_row // length, axis=1)
    return rep.reshape(length, n_row, rows).transpose(1, 0, 2).astype(np.float32)


def kernel(
    n_row, n_col, obs, est, bank, ids, wts, ill_here, spread, moves, inv_all, out,
    ext, ystrip, strips, corn, cornsend, plane, ids_z, sel_send, sel_recv, ill, inv,
    base, rt, ctc, cth, ptc, pth, cur, obs_t, rfac,
    local_sem, psend, precv, isend, irecv, bsend, brecv, lsend, lrecv, hsend, hrecv,
):
    depth = obs.shape[0]
    groups = depth // GZ
    planes = n_col // 4
    row = lax.axis_index("row")
    col = lax.axis_index("col")
    zc = col // 4
    slot = lax.rem(col, 4)
    core_col = zc * 4 + slot + 1 - 2 * lax.rem(slot, 2)
    x_slot = lax.rem(slot + 2, 4)
    x_col = zc * 4 + x_slot

    def z_col(d):
        return lax.rem(zc + d + planes, planes) * 4 + slot

    up, down = lax.rem(row + n_row - 1, n_row), lax.rem(row + 1, n_row)
    left, right = lax.rem(col + n_col - 1, n_col), lax.rem(col + 1, n_col)

    inv_copy = pltpu.make_async_copy(inv_all.at[row], inv, local_sem)
    inv_copy.start()

    for p in range(4):
        ext[p, :, 128:160, :] = jnp.zeros((depth, 32, 256), BF)
    ystrip[...] = jnp.zeros_like(ystrip)
    corn[...] = jnp.zeros_like(corn)

    barrier = pltpu.get_barrier_semaphore()
    friends = [(row, z_col(d)) for d in range(1, planes)]
    friends += [(row, core_col), (row, x_col)]
    friends += [(lax.rem(row + d, n_row), col) for d in range(1, n_row)]
    friends += [(row, left), (row, right)]
    friends += [(up, left), (up, right), (down, left), (down, right)]
    for friend in friends:
        pl.semaphore_signal(barrier, inc=1, device_id=friend, device_id_type=MESH)
    pl.semaphore_wait(barrier, len(friends))

    def remote(src, dst, s, r, to):
        return pltpu.make_async_remote_copy(
            src_ref=src, dst_ref=dst, send_sem=s, recv_sem=r, device_id=to, device_id_type=MESH
        )

    x_copy = remote(bank, plane.at[slot], psend.at[0], precv.at[0], (row, x_col))
    core_copy = remote(bank, plane.at[slot], psend.at[1], precv.at[1], (row, core_col))
    x_copy.start()
    core_copy.start()
    id_copies = [
        remote(ids, ids_z.at[d], isend.at[d], irecv.at[d], (row, z_col(-d))) for d in range(1, planes)
    ]
    for c in id_copies:
        c.start()
    ill_copies = [
        remote(
            ill_here, ill.at[pl.ds(row * 16, 16)], lsend.at[d], lrecv.at[d], (lax.rem(row + d, n_row), col)
        )
        for d in range(1, n_row)
    ]
    for c in ill_copies:
        c.start()
    plane[slot] = bank[...]
    ids_z[0] = ids[...]
    ill[pl.ds(row * 16, 16)] = ill_here[...]

    has = {"u": row > 0, "d": row < n_row - 1, "l": col > 0, "r": col < n_col - 1}

    def halo_copies(p, g):
        zs = pl.ds(g * GZ, GZ)
        top, bottom = pl.ds(0, 16), pl.ds(16, 16)
        mid = pl.ds(0, 128)
        plan = [
            ("l", ext.at[p, zs, pl.ds(0, 16), mid], ext.at[p, zs, pl.ds(128, 16), mid], (row, left)),
            ("r", ext.at[p, zs, pl.ds(112, 16), mid], ext.at[p, zs, pl.ds(144, 16), mid], (row, right)),
            ("u", strips.at[p, zs, top], ystrip.at[p, zs, top], (up, col)),
            ("d", strips.at[p, zs, bottom], ystrip.at[p, zs, bottom], (down, col)),
            ("ul", cornsend.at[p, g, top], corn.at[p, g, 0, top], (up, left)),
            ("dl", cornsend.at[p, g, bottom], corn.at[p, g, 0, bottom], (down, left)),
            ("ur", cornsend.at[p, g, top], corn.at[p, g, 1, top], (up, right)),
            ("dr", cornsend.at[p, g, bottom], corn.at[p, g, 1, bottom], (down, right)),
        ]
        return [
            (where, remote(src, dst, hsend.at[p, g, i], hrecv.at[p, g, i], to))
            for i, (where, src, dst, to) in enumerate(plan)
        ]

    opposite = {"u": "d", "d": "u", "l": "r", "r": "l"}

    def there(where):
        ok = has[where[0]]
        for w in where[1:]:
            ok = jnp.logical_and(ok, has[w])
        return ok

    def halo_start(p, g):
        for where, c in halo_copies(p, g):
            @pl.when(there(where))
            def _():
                c.start()

    def halo_wait_recv(p, g):
        for where, c in halo_copies(p, g):
            @pl.when(there("".join(opposite[w] for w in where)))
            def _():
                c.wait_recv()

    def halo_wait_send(p, g):
        for where, c in halo_copies(p, g):
            @pl.when(there(where))
            def _():
                c.wait_send()

    def place_at(zz):
        return moves[160 + zz * 128 : 288 + zz * 128]

    def strip_of(p, z, field_b):
        ext[p, z, 0:128, 0:128] = field_b
        s = mm_nt(moves[128:160], field_b).astype(BF)
        strips[p, z] = s
        return s

    @pl.loop(0, groups)
    def _(g):
        acc = jnp.zeros((32, 128), F32)
        for zz in range(GZ):
            z = g * GZ + zz
            c = jnp.transpose(est[z])
            cur[z] = c
            obs_t[z] = jnp.transpose(obs[z])
            acc = acc + mm(strip_of(0, z, c.astype(BF)), place_at(zz))
        cornsend[0, g] = acc.astype(BF)
        halo_start(0, g)

    x_copy.wait_recv()
    forward = remote(plane.at[x_slot], plane.at[x_slot], psend.at[2], precv.at[2], (row, core_col))
    forward.start()
    core_copy.wait_recv()
    for c in id_copies:
        c.wait_recv()
    forward.wait_recv()

    def selection(d):
        for k in range(2):
            mine = ids_z[d, k].astype(F32)
            picked = [jnp.zeros((depth, 128), F32) for _ in range(4)]
            for s in range(4):
                for i in range(4):
                    zone = (zc * 16 + s * 4 + i).astype(F32)
                    hit = mine == zone
                    for q in range(4):
                        picked[q] = jnp.where(hit, plane[s, i, q].astype(F32), picked[q])
            for q in range(4):
                sel_send[d, k * 4 + q] = picked[q].astype(BF)

    sel_copies = [
        remote(sel_send.at[d], sel_recv.at[d], bsend.at[d], brecv.at[d], (row, z_col(d)))
        for d in range(1, planes)
    ]
    for d in range(1, planes):
        selection(d)
        sel_copies[d - 1].start()
    selection(0)

    inv_copy.wait()
    for c in ill_copies:
        c.wait_recv()
    fac = jnp.dot(
        jnp.transpose(ill[...])[0:depth], inv[...], precision=lax.Precision.HIGHEST,
        preferred_element_type=F32,
    )
    rfac[...] = 1.0 / fac

    for c in sel_copies:
        c.wait_recv()
    total = jnp.zeros((depth, 128), F32)
    for j in range(8):
        s = sel_send[0, j].astype(F32)
        for d in range(1, planes):
            s = s + sel_recv[d, j].astype(F32)
        b = mm(s.astype(BF), spread[...])
        total = total + wts[j // 4] * b[:, 512:640] * b[:, 640:768]
        for t in range(4):
            base[t, j] = b[:, t * 128 : (t + 1) * 128]
    for j in range(8):
        for t in range(2):
            base[t, j] = (wts[j // 4] * base[t, j]) / total

    lanes = lax.broadcasted_iota(jnp.int32, (16, 128), 1)
    low = lanes < 64

    def circulant(t, j, z):
        b = jnp.broadcast_to(base[t, j, pl.ds(z, 1), :], (128, 128))
        return pltpu.roll(b, 0, 1, stride=1, stride_axis=0)

    def build(way, z):
        zero = jnp.zeros((16, 128), F32)
        left_h = [zero, zero]
        right_h = [zero, zero]
        for j in range(8):
            js = slice(j * 128, (j + 1) * 128)
            r = circulant(way, j, z)
            first, last = r[0:16], r[112:128]
            rt[way, z, 0:16, js] = jnp.where(low, first, 0.0).astype(BF)
            rt[way, z, 16:112, js] = r[16:112].astype(BF)
            rt[way, z, 112:128, js] = jnp.where(low, 0.0, last).astype(BF)
            rt[way, z, 128:144, js] = jnp.where(low, 0.0, first).astype(BF)
            rt[way, z, 144:160, js] = jnp.where(low, last, 0.0).astype(BF)
            c = circulant(2 + way, j, z)
            first, last = c[0:16], c[112:128]
            ctc[way, z, 0:16, js] = jnp.where(low, first, 0.0).astype(BF)
            ctc[way, z, 16:112, js] = c[16:112].astype(BF)
            ctc[way, z, 112:128, js] = jnp.where(low, 0.0, last).astype(BF)
            at = (j % 4) * 32
            left_h[j // 4] += pltpu.roll(jnp.where(low, 0.0, first), (at + 16 + 16) % 128, 1)
            right_h[j // 4] += pltpu.roll(jnp.where(low, last, 0.0), at, 1)
        for h in range(2):
            hs = slice(h * 128, (h + 1) * 128)
            cth[way, z, 0:16, hs] = left_h[h].astype(BF)
            cth[way, z, 16:112, hs] = jnp.zeros((96, 128), BF)
            cth[way, z, 112:128, hs] = right_h[h].astype(BF)

    def blur(p, z, zz, corner_r, corner_l):
        way = p % 2
        ext[p, z, 0:128, 128:160] = mm_nt(moves[0:128], ystrip[p, z]).astype(BF)
        ext[p, z, 128:144, 128:160] = corner_r[zz * 16 : zz * 16 + 16]
        ext[p, z, 144:160, 128:160] = corner_l[zz * 16 : zz * 16 + 16]
        field = ext[p, z, :, 0:160]
        for jp in range(4):
            o = mm(field, rt[way, z, :, jp * 256 : (jp + 1) * 256]).astype(BF)
            for h in range(2):
                j = jp * 2 + h
                ptc[zz, j * 128 : (j + 1) * 128] = o[0:128, h * 128 : (h + 1) * 128]
                pth[zz, j * 32 : (j + 1) * 32] = o[128:160, h * 128 : (h + 1) * 128]
        return mm(ctc[way, z], ptc[zz]) + mm(cth[way, z], pth[zz])

    first_sel = 160 + GZ * 128
    for p in range(4):
        @pl.loop(0, groups)
        def _(g):
            if p < 2:
                @pl.loop(0, GZ)
                def _(zz):
                    build(p, g * GZ + zz)
            halo_wait_recv(p, g)
            corner_r = mm_nt(moves[first_sel : first_sel + GZ * 16], corn[p, g, 0]).astype(BF)
            corner_l = mm_nt(moves[first_sel + GZ * 16 : first_sel + 2 * GZ * 16], corn[p, g, 1]).astype(BF)
            acc = jnp.zeros((32, 128), F32)
            for zz in range(GZ):
                z = g * GZ + zz
                f = blur(p, z, zz, corner_r, corner_l)
                if p % 2 == 0:
                    field = (obs_t[z] / f).astype(BF)
                else:
                    new = cur[z] * f * rfac[pl.ds(z, 1), :]
                    if p == 3:
                        out[z] = jnp.transpose(new)
                        continue
                    cur[z] = new
                    field = new.astype(BF)
                acc = acc + mm(strip_of(p + 1, z, field), place_at(zz))
            if p < 3:
                cornsend[p + 1, g] = acc.astype(BF)
                halo_start(p + 1, g)

    x_copy.wait_send()
    core_copy.wait_send()
    forward.wait_send()
    for c in id_copies + ill_copies + sel_copies:
        c.wait_send()
    for p in range(4):
        @pl.loop(0, groups)
        def _(g):
            halo_wait_send(p, g)


def shards(n_row, n_col, observed, estimate, psf_bank, zone_ids, mix_weights, illumination):
    depth, rows, cols = estimate.shape
    zones = psf_bank.shape[0]
    groups = depth // GZ
    planes = n_col // 4
    cells = psf_bank.transpose(2, 0, 3, 1, 4)
    row_f, col_f = cells[0], cells[1]

    def high(v):
        return lax.reduce_precision(v, 8, 7)

    sums = jnp.sum(col_f, -1, keepdims=True)
    r_hi = high(row_f)
    s_hi = high(sums)
    s_mid = high(sums - s_hi)
    bank = jnp.concatenate(
        [r_hi, row_f - r_hi, col_f, s_hi, s_mid, sums - s_hi - s_mid,
         jnp.zeros((zones, 4, depth, 128 - 3 * TAPS - 3), F32)], -1,
    ).astype(BF)
    ids = jnp.broadcast_to(zone_ids[0, 0].T[:, :, None], (2, depth, 128)).astype(BF)
    wts = jnp.broadcast_to(mix_weights[0, 0].T[:, :, None], (2, depth, 128))
    ill_here = jnp.pad(illumination[:, :, 0].T, ((0, 0), (0, 128 - depth)))
    length = illumination.shape[1] * n_row
    spread = jnp.asarray(spread_table())
    moves = jnp.asarray(moves_table())
    inv_all = jnp.asarray(smoothing_table(length, n_row, rows))
    vmem = pl.BlockSpec(memory_space=pltpu.VMEM)
    dma = pltpu.SemaphoreType.DMA
    return pl.pallas_call(
        functools.partial(kernel, n_row, n_col),
        out_shape=jax.ShapeDtypeStruct(estimate.shape, F32),
        in_specs=[vmem] * 8 + [pl.BlockSpec(memory_space=pl.ANY)],
        out_specs=vmem,
        scratch_shapes=[
            pltpu.VMEM((4, depth, 160, 256), BF),
            pltpu.VMEM((4, depth, 32, 128), BF),
            pltpu.VMEM((4, depth, 32, 128), BF),
            pltpu.VMEM((4, groups, 2, 32, 128), BF),
            pltpu.VMEM((4, groups, 32, 128), BF),
            pltpu.VMEM((4, zones, 4, depth, 128), BF),
            pltpu.VMEM((planes, 2, depth, 128), BF),
            pltpu.VMEM((planes, 8, depth, 128), BF),
            pltpu.VMEM((planes, 8, depth, 128), BF),
            pltpu.VMEM((length, 128), F32),
            pltpu.VMEM((length, rows), F32),
            pltpu.VMEM((4, 8, depth, 128), F32),
            pltpu.VMEM((2, depth, 160, 1024), BF),
            pltpu.VMEM((2, depth, 128, 1024), BF),
            pltpu.VMEM((2, depth, 128, 256), BF),
            pltpu.VMEM((GZ, 1024, 128), BF),
            pltpu.VMEM((GZ, 256, 128), BF),
            pltpu.VMEM((depth, 128, 128), F32),
            pltpu.VMEM((depth, 128, 128), F32),
            pltpu.VMEM((depth, 128), F32),
            dma,
            dma((3,)), dma((3,)),
            dma((planes,)), dma((planes,)),
            dma((planes,)), dma((planes,)),
            dma((n_row,)), dma((n_row,)),
            dma((4, groups, 8)), dma((4, groups, 8)),
        ],
        compiler_params=pltpu.CompilerParams(
            collective_id=0, has_side_effects=True, vmem_limit_bytes=60 * 2**20
        ),
        name="deconvolve",
    )(observed, estimate, bank, ids, wts, ill_here, spread, moves, inv_all)


def solution(mesh):
    placed = (
        P(None, "row", "col"),
        P(None, "row", "col"),
        P(("row", "col"), None, None, None, None),
        P("row", "col", None, None),
        P("row", "col", None, None),
        P(None, "row", "col"),
    )
    return jax.shard_map(
        functools.partial(shards, mesh.shape["row"], mesh.shape["col"]),
        mesh=mesh, in_specs=placed, out_specs=P(None, "row", "col"), check_vma=False,
    )
```

profile of v0, /device:TPU:1, one launch (start us, length us, event | category | flops | bytes accessed | tf_op | source)
XLA Modules:
  0.0 98.1 jit_solution(4326422925919895152)
XLA Ops:
  0.0 0.0 copy-start
  0.0 0.7 convert_bitcast_fusion
  0.7 0.7 broadcast_in_dim.7.ids
  1.4 0.0 copy-done
  1.4 0.1 copy.21
  1.5 0.0 copy-start.1
  1.5 0.6 pad.4.ill_here
  2.1 0.1 copy-done.1
  2.1 0.7 broadcast_in_dim.8.wts
  2.8 1.0 %copy.23 = f32[4,16,2,4,33]{4,1,3,0,2:T(8,128)S(1)} copy(f32[4,16,2,4,33]{4,3,2,1,0:T(4,128)} %param.11) | data formatting | bytes 135168 | tf_op args[2]
  3.8 0.1 slice_reduce_fusion
  3.9 0.2 copy.20
  4.2 0.2 copy.19
  4.4 0.2 copy.18
  4.6 0.8 concatenate.4.bank
  5.4 90.4 %deconvolve.1 = f32[16,128,128]{2,1,0:T(8,128)} custom-call(f32[16,128,128]{2,1,0:T(8,128)} %obs.1, f32[16,128,128]{2,1,0:T(8,128)} %est.1, bf16[4,4,16,128]{3,2,1,0:T(8,128)(2,1)} %concatenate.4.bank, bf16[2,16,128]{2,1,0:T(8,128)(2,1)} %broadcast_in_dim.7.ids, f32[2,16,128]{2,1,0:T(8,128)} %broadcast_in_dim.8.wts, f32[16,128]{1,0:T(8,128)} %pad.4.ill_here, ...), custom_call_target="tpu_custom_call" | custom-call | tf_op jit(solution)/shard_map/deconvolve/pallas_call | solution.py:370
  95.8 2.3 %copy.25 = f32[16,128,128]{2,1,0:T(8,128)} copy(f32[16,128,128]{2,1,0:T(8,128)} %deconvolve.1) | data formatting | bytes 2097152
  (5 shorter events, 0.1 us)
Async XLA Ops:
  0.0 1.4 %copy-start = (f32[16,16,1]{1,2,0:T(1,128)S(1)}, f32[16,16,1]{1,2,0:T(1,128)}, u32[]{:S(2)}) copy-start(f32[16,16,1]{1,2,0:T(1,128)} %param.14) | copy-start | bytes 3076
  1.5 0.7 copy-start.1
where the time goes:
time: 98.3 us; the launch traced here: 98.1 us
  Pallas kernels  90.4 us (92%)
  local copies, waits for them, and re-layouts  6.79 us (7%)
    pallas_call x1, Pallas kernels, shards(): pl.pallas_call(functools.partial(kernel, n_row, n_col), out_shape=jax.Sha...  90.4 us
    unnamed x7, local copies, waits for them, and re-layouts  3.45 us

commit v1 on v0

v1 whole, which is shorter than its diff:
```python
import functools

import jax
import jax.numpy as jnp
import numpy as np
from jax import lax
from jax.experimental import pallas as pl
from jax.experimental.pallas import tpu as pltpu
from jax.sharding import PartitionSpec as P

MESH = pl.DeviceIdType.MESH
BF = jnp.bfloat16
F32 = jnp.float32
TAPS = 33
HALF = 16
GZ = 4
NT = (((1,), (1,)), ((), ()))


def mm(a, b):
    return jnp.dot(a, b, preferred_element_type=F32)


def mm_nt(a, b):
    return lax.dot_general(a, b, NT, preferred_element_type=F32)


def spread_table():
    w = np.zeros((128, 6 * 128), np.float32)
    for a in range(TAPS):
        plus, minus = (a - HALF) % 128, (HALF - a) % 128
        for lane in (a, TAPS + a):
            w[lane, minus] = 1.0
            w[lane, 128 + plus] = 1.0
            w[lane, 512:640] = 1.0
        w[2 * TAPS + a, 256 + plus] = 1.0
        w[2 * TAPS + a, 384 + minus] = 1.0
    w[3 * TAPS : 3 * TAPS + 3, 640:768] = 1.0
    return w.astype(BF)


def moves_table():
    eye = np.eye(128, dtype=np.float32)
    ends = np.concatenate([eye[:16], eye[112:]], 0)
    sel_r = np.zeros((GZ * 16, 128), np.float32)
    sel_l = np.zeros((GZ * 16, 128), np.float32)
    for zz in range(GZ):
        for i in range(16):
            sel_l[zz * 16 + i, zz * 32 + i] = 1.0
            sel_r[zz * 16 + i, zz * 32 + 16 + i] = 1.0
    none = np.zeros_like(sel_r)
    sel = np.block([[sel_r, none], [none, sel_l]])
    return np.concatenate([eye, ends], 0).astype(BF), sel.astype(BF)


def smoothing_table(length, n_row, rows):
    stiff = float(length * length) / 16.0
    d = np.diff(np.eye(length), axis=0)
    inv = np.linalg.inv(np.eye(length) + stiff * d.T @ d)
    rep = np.repeat(inv, rows * n_row // length, axis=1)
    return rep.reshape(length, n_row, rows).transpose(1, 0, 2).astype(np.float32)


def kernel(
    n_row, n_col, cells, ids_in, wts_in, ill_in, spread, moves, picks, obs_hbm, est_hbm, inv_all, out_hbm,
    obs, est, out, wide, bank, ids, wts, ill_here, ext0, ext1, ext2, ext3, ystrip, strips, corn, cornsend, plane, ids_z, sel_send, sel_recv, ill, inv,
    base, rt0, rt1, ctc0, ctc1, cth0, cth1, ptc, pth, cur, obs_t, rfac,
    local_sem, est_sem, obs_sem, out_sem, psend, precv, isend, irecv, bsend, brecv, lsend, lrecv, hsend, hrecv,
):
    ext = (ext0, ext1, ext2, ext3)
    rt, ctc, cth = (rt0, rt1), (ctc0, ctc1), (cth0, cth1)
    depth = obs.shape[0]
    groups = depth // GZ
    planes = n_col // 4
    row = lax.axis_index("row")
    col = lax.axis_index("col")
    zc = col // 4
    slot = lax.rem(col, 4)
    core_col = zc * 4 + slot + 1 - 2 * lax.rem(slot, 2)
    x_slot = lax.rem(slot + 2, 4)
    x_col = zc * 4 + x_slot

    def z_col(d):
        return lax.rem(zc + d + planes, planes) * 4 + slot

    up, down = lax.rem(row + n_row - 1, n_row), lax.rem(row + 1, n_row)
    left, right = lax.rem(col + n_col - 1, n_col), lax.rem(col + 1, n_col)

    inv_copy = pltpu.make_async_copy(inv_all.at[row], inv, local_sem)
    inv_copy.start()
    est_copy = pltpu.make_async_copy(est_hbm, est, est_sem)
    est_copy.start()
    obs_copy = pltpu.make_async_copy(obs_hbm, obs, obs_sem)
    obs_copy.start()
    zones = cells.shape[1]
    lane = lax.broadcasted_iota(jnp.int32, (depth, 128), 1)
    wide[...] = jnp.zeros_like(wide)
    wide[:, :, :, :, 0:TAPS] = cells[...]
    for i in range(zones):
        for q in range(4):
            r, c = wide[0, i, q], wide[1, i, q]
            r_hi = r.astype(BF).astype(F32)
            total_c = jnp.sum(c, -1, keepdims=True)
            s_hi = total_c.astype(BF).astype(F32)
            s_mid = (total_c - s_hi).astype(BF).astype(F32)
            packed = r_hi + pltpu.roll(r - r_hi, TAPS, 1) + pltpu.roll(c, 2 * TAPS, 1)
            packed = jnp.where(lane == 3 * TAPS, s_hi, packed)
            packed = jnp.where(lane == 3 * TAPS + 1, s_mid, packed)
            packed = jnp.where(lane == 3 * TAPS + 2, total_c - s_hi - s_mid, packed)
            bank[i, q] = packed.astype(BF)
    for k in range(2):
        ids[k] = jnp.transpose(jnp.broadcast_to(ids_in[k : k + 1].astype(F32), (128, depth))).astype(BF)
        wts[k] = jnp.transpose(jnp.broadcast_to(wts_in[k : k + 1], (128, depth)))
    ill_here[...] = jnp.zeros_like(ill_here)
    ill_here[:, 0 : ill_in.shape[1]] = ill_in[...]

    for p in range(4):
        ext[p][:, 128:160, :] = jnp.zeros((depth, 32, 256), BF)
    ystrip[...] = jnp.zeros_like(ystrip)
    corn[...] = jnp.zeros_like(corn)

    barrier = pltpu.get_barrier_semaphore()
    friends = [(row, z_col(d)) for d in range(1, planes)]
    friends += [(row, core_col), (row, x_col)]
    friends += [(lax.rem(row + d, n_row), col) for d in range(1, n_row)]
    friends += [(row, left), (row, right)]
    friends += [(up, left), (up, right), (down, left), (down, right)]
    for friend in friends:
        pl.semaphore_signal(barrier, inc=1, device_id=friend, device_id_type=MESH)
    pl.semaphore_wait(barrier, len(friends))

    def remote(src, dst, s, r, to):
        return pltpu.make_async_remote_copy(
            src_ref=src, dst_ref=dst, send_sem=s, recv_sem=r, device_id=to, device_id_type=MESH
        )

    x_copy = remote(bank, plane.at[slot], psend.at[0], precv.at[0], (row, x_col))
    core_copy = remote(bank, plane.at[slot], psend.at[1], precv.at[1], (row, core_col))
    x_copy.start()
    core_copy.start()
    id_copies = [
        remote(ids, ids_z.at[d], isend.at[d], irecv.at[d], (row, z_col(-d))) for d in range(1, planes)
    ]
    for c in id_copies:
        c.start()
    ill_copies = [
        remote(
            ill_here, ill.at[row], lsend.at[d], lrecv.at[d], (lax.rem(row + d, n_row), col)
        )
        for d in range(1, n_row)
    ]
    for c in ill_copies:
        c.start()
    plane[slot] = bank[...]
    ids_z[0] = ids[...]
    ill[row] = ill_here[...]

    has = {"u": row > 0, "d": row < n_row - 1, "l": col > 0, "r": col < n_col - 1}

    def halo_copies(p, g):
        zs = pl.ds(g * GZ, GZ)
        top, bottom = pl.ds(0, 16), pl.ds(16, 16)
        mid = pl.ds(0, 128)
        plan = [
            ("l", ext[p].at[zs, pl.ds(0, 16), mid], ext[p].at[zs, pl.ds(128, 16), mid], (row, left)),
            ("r", ext[p].at[zs, pl.ds(112, 16), mid], ext[p].at[zs, pl.ds(144, 16), mid], (row, right)),
            ("u", strips.at[p, zs, top], ystrip.at[p, zs, top], (up, col)),
            ("d", strips.at[p, zs, bottom], ystrip.at[p, zs, bottom], (down, col)),
            ("ul", cornsend.at[p, g, top], corn.at[p, g, top, pl.ds(0, 128)], (up, left)),
            ("dl", cornsend.at[p, g, bottom], corn.at[p, g, bottom, pl.ds(0, 128)], (down, left)),
            ("ur", cornsend.at[p, g, top], corn.at[p, g, top, pl.ds(128, 128)], (up, right)),
            ("dr", cornsend.at[p, g, bottom], corn.at[p, g, bottom, pl.ds(128, 128)], (down, right)),
        ]
        return [
            (where, remote(src, dst, hsend.at[p, g, i], hrecv.at[p, g, i], to))
            for i, (where, src, dst, to) in enumerate(plan)
        ]

    opposite = {"u": "d", "d": "u", "l": "r", "r": "l"}

    def there(where):
        ok = has[where[0]]
        for w in where[1:]:
            ok = jnp.logical_and(ok, has[w])
        return ok

    def halo_start(p, g):
        for where, c in halo_copies(p, g):
            @pl.when(there(where))
            def _():
                c.start()

    def halo_wait_recv(p, g):
        for where, c in halo_copies(p, g):
            @pl.when(there("".join(opposite[w] for w in where)))
            def _():
                c.wait_recv()

    def halo_wait_send(p, g):
        for where, c in halo_copies(p, g):
            @pl.when(there(where))
            def _():
                c.wait_send()

    quarter = lax.broadcasted_iota(jnp.int32, (32, 128), 1) // 32

    def pack(p, g, fields):
        for zz in range(GZ):
            ext[p][g * GZ + zz, 0:128, 0:128] = fields[zz]
        s = mm_nt(moves[128:160], jnp.concatenate(fields, 0)).astype(BF)
        for zz in range(GZ):
            strips[p, g * GZ + zz] = s[:, zz * 128 : (zz + 1) * 128]
        c = jnp.zeros((32, 128), F32)
        for zz in range(GZ):
            turned = pltpu.roll(s[:, zz * 128 : (zz + 1) * 128].astype(F32), 16 + zz * 32, 1)
            c = jnp.where(quarter == zz, turned, c)
        cornsend[p, g] = c.astype(BF)
        halo_start(p, g)

    est_copy.wait()

    @pl.loop(0, groups)
    def _(g):
        fields = []
        for zz in range(GZ):
            z = g * GZ + zz
            c = jnp.transpose(est[z])
            cur[z] = c
            fields.append(c.astype(BF))
        pack(0, g, fields)

    x_copy.wait_recv()
    forward = remote(plane.at[x_slot], plane.at[x_slot], psend.at[2], precv.at[2], (row, core_col))
    forward.start()
    core_copy.wait_recv()
    for c in id_copies:
        c.wait_recv()
    forward.wait_recv()

    def selection(d):
        for k in range(2):
            mine = ids_z[d, k].astype(F32)
            picked = [jnp.zeros((depth, 128), F32) for _ in range(4)]
            for s in range(4):
                for i in range(4):
                    zone = (zc * 16 + s * 4 + i).astype(F32)
                    hit = mine == zone
                    for q in range(4):
                        picked[q] = jnp.where(hit, plane[s, i, q].astype(F32), picked[q])
            for q in range(4):
                sel_send[d, k * 4 + q] = picked[q].astype(BF)

    sel_copies = [
        remote(sel_send.at[d], sel_recv.at[d], bsend.at[d], brecv.at[d], (row, z_col(d)))
        for d in range(1, planes)
    ]
    for d in range(1, planes):
        selection(d)
        sel_copies[d - 1].start()
    selection(0)

    inv_copy.wait()
    for c in ill_copies:
        c.wait_recv()
    coarse = ill_in.shape[1]
    fac = jnp.zeros((depth, inv.shape[1]), F32)
    for i in range(n_row):
        fac = fac + jnp.dot(
            ill[i, :, 0:coarse], inv[i * coarse : (i + 1) * coarse],
            precision=lax.Precision.HIGHEST, preferred_element_type=F32,
        )
    rfac[...] = 1.0 / fac

    obs_copy.wait()
    for c in sel_copies:
        c.wait_recv()
    picked = sel_send[0].astype(F32)
    for d in range(1, planes):
        picked = picked + sel_recv[d].astype(F32)
    b = mm(jnp.reshape(picked, (8 * depth, 128)).astype(BF), spread[...])
    total = jnp.zeros((depth, 128), F32)
    for j in range(8):
        r = b[j * depth : (j + 1) * depth]
        total = total + wts[j // 4] * r[:, 512:640] * r[:, 640:768]
    for j in range(8):
        r = b[j * depth : (j + 1) * depth]
        for t in range(4):
            v = r[:, t * 128 : (t + 1) * 128]
            base[t, j] = (wts[j // 4] * v) / total if t < 2 else v

    low = lax.broadcasted_iota(jnp.int32, (16, 128), 1) < 64
    lower = low.astype(F32).astype(BF)
    upper = 1.0 - lower

    def circulant(t, j, z):
        b = jnp.broadcast_to(base[t, j, pl.ds(z, 1), :], (16, 128))
        b = pltpu.roll(b, 0, 1, stride=1, stride_axis=0).astype(BF)
        return [pltpu.roll(b, 16 * i, 1) if i else b for i in range(8)]

    def build(way, z):
        left_h = [0.0, 0.0]
        right_h = [0.0, 0.0]
        for j in range(8):
            js = slice(j * 128, (j + 1) * 128)
            r = circulant(way, j, z)
            c = circulant(2 + way, j, z)
            for i in range(1, 7):
                rt[way][z, i * 16 : i * 16 + 16, js] = r[i]
                ctc[way][z, i * 16 : i * 16 + 16, js] = c[i]
            rt[way][z, 0:16, js] = r[0] * lower
            rt[way][z, 112:128, js] = r[7] * upper
            rt[way][z, 128:144, js] = r[0] * upper
            rt[way][z, 144:160, js] = r[7] * lower
            ctc[way][z, 0:16, js] = c[0] * lower
            ctc[way][z, 112:128, js] = c[7] * upper
            at = (j % 4) * 32
            left_h[j // 4] += pltpu.roll(c[0] * upper, (at + 16 + 16) % 128, 1)
            right_h[j // 4] += pltpu.roll(c[7] * lower, at, 1) if at else c[7] * lower
        for h in range(2):
            hs = slice(h * 128, (h + 1) * 128)
            cth[way][z, 0:16, hs] = left_h[h]
            cth[way][z, 16:112, hs] = jnp.zeros((96, 128), BF)
            cth[way][z, 112:128, hs] = right_h[h]

    def out_copy(g):
        zs = pl.ds(g * GZ, GZ)
        return pltpu.make_async_copy(out.at[zs], out_hbm.at[zs], out_sem.at[g])

    def unpack(p, g):
        edges = jnp.reshape(ystrip[p, pl.ds(g * GZ, GZ)], (GZ * 32, 128))
        mid = mm_nt(moves[0:128], edges)
        corner = mm_nt(picks[...], corn[p, g]).astype(BF)
        for zz in range(GZ):
            z = g * GZ + zz
            turned = pltpu.roll(mid, 128 - zz * 32, 1) if zz else mid
            ext[p][z, 0:128, 128:160] = turned[:, 0:32].astype(BF)
            at = zz * 16
            ext[p][z, 128:144, 128:160] = corner[at : at + 16]
            at = (GZ + zz) * 16
            ext[p][z, 144:160, 128:160] = corner[at : at + 16]

    def rows_stage(p, z, zz):
        field = ext[p][z, :, 0:160]
        for jp in range(4):
            o = mm(field, rt[p % 2][z, :, jp * 256 : (jp + 1) * 256]).astype(BF)
            for h in range(2):
                j = jp * 2 + h
                ptc[zz, j * 128 : (j + 1) * 128] = o[0:128, h * 128 : (h + 1) * 128]
                pth[zz, j * 32 : (j + 1) * 32] = o[128:160, h * 128 : (h + 1) * 128]

    def cols_stage(p, z, zz):
        return mm(ctc[p % 2][z], ptc[zz]) + mm(cth[p % 2][z], pth[zz])

    for p in range(4):
        @pl.loop(0, groups)
        def _(g):
            if p < 2:
                @pl.loop(0, GZ)
                def _(zz):
                    build(p, g * GZ + zz)
            halo_wait_recv(p, g)
            unpack(p, g)
            fields = []
            for step in range(GZ + 1):
                if step < GZ:
                    rows_stage(p, g * GZ + step, step)
                if step == 0:
                    continue
                zz = step - 1
                z = g * GZ + zz
                f = cols_stage(p, z, zz)
                if p % 2 == 0:
                    fields.append((jnp.transpose(obs[z]) / f if p == 0 else obs_t[z] / f).astype(BF))
                    if p == 0:
                        obs_t[z] = jnp.transpose(obs[z])
                else:
                    new = cur[z] * f * rfac[pl.ds(z, 1), :]
                    if p == 3:
                        out[z] = jnp.transpose(new)
                    else:
                        cur[z] = new
                        fields.append(new.astype(BF))
            if p < 3:
                pack(p + 1, g, fields)
            else:
                out_copy(g).start()

    x_copy.wait_send()
    core_copy.wait_send()
    forward.wait_send()
    for c in id_copies + ill_copies + sel_copies:
        c.wait_send()
    for g in range(groups):
        out_copy(g).wait()
    for p in range(4):
        @pl.loop(0, groups)
        def _(g):
            halo_wait_send(p, g)


def shards(n_row, n_col, observed, estimate, psf_bank, zone_ids, mix_weights, illumination):
    depth, rows, cols = estimate.shape
    zones = psf_bank.shape[0]
    groups = depth // GZ
    planes = n_col // 4
    cells = psf_bank.transpose(2, 0, 3, 1, 4)
    ids = zone_ids[0, 0].T
    wts = mix_weights[0, 0].T
    ill_here = illumination[:, :, 0]
    length = illumination.shape[1] * n_row
    spread = jnp.asarray(spread_table())
    moves, picks = map(jnp.asarray, moves_table())
    inv_all = jnp.asarray(smoothing_table(length, n_row, rows))
    vmem = pl.BlockSpec(memory_space=pltpu.VMEM)
    hbm = pl.BlockSpec(memory_space=pl.ANY)
    dma = pltpu.SemaphoreType.DMA
    return pl.pallas_call(
        functools.partial(kernel, n_row, n_col),
        out_shape=jax.ShapeDtypeStruct(estimate.shape, F32),
        in_specs=[vmem] * 7 + [hbm] * 3,
        out_specs=hbm,
        scratch_shapes=[
            *[pltpu.VMEM((depth, rows, cols), F32)] * 3,
            pltpu.VMEM((2, zones, 4, depth, 128), F32),
            pltpu.VMEM((zones, 4, depth, 128), BF),
            pltpu.VMEM((2, depth, 128), BF),
            pltpu.VMEM((2, depth, 128), F32),
            pltpu.VMEM((depth, 128), F32),
            *[pltpu.VMEM((depth, 160, 256), BF)] * 4,
            pltpu.VMEM((4, depth, 32, 128), BF),
            pltpu.VMEM((4, depth, 32, 128), BF),
            pltpu.VMEM((4, groups, 32, 256), BF),
            pltpu.VMEM((4, groups, 32, 128), BF),
            pltpu.VMEM((4, zones, 4, depth, 128), BF),
            pltpu.VMEM((planes, 2, depth, 128), BF),
            pltpu.VMEM((planes, 8, depth, 128), BF),
            pltpu.VMEM((planes, 8, depth, 128), BF),
            pltpu.VMEM((n_row, depth, 128), F32),
            pltpu.VMEM((length, rows), F32),
            pltpu.VMEM((4, 8, depth, 128), F32),
            *[pltpu.VMEM((depth, 160, 1024), BF)] * 2,
            *[pltpu.VMEM((depth, 128, 1024), BF)] * 2,
            *[pltpu.VMEM((depth, 128, 256), BF)] * 2,
            pltpu.VMEM((GZ, 1024, 128), BF),
            pltpu.VMEM((GZ, 256, 128), BF),
            pltpu.VMEM((depth, 128, 128), F32),
            pltpu.VMEM((depth, 128, 128), F32),
            pltpu.VMEM((depth, 128), F32),
            dma, dma, dma, dma((groups,)),
            dma((3,)), dma((3,)),
            dma((planes,)), dma((planes,)),
            dma((planes,)), dma((planes,)),
            dma((n_row,)), dma((n_row,)),
            dma((4, groups, 8)), dma((4, groups, 8)),
        ],
        compiler_params=pltpu.CompilerParams(
            collective_id=0, has_side_effects=True, vmem_limit_bytes=60 * 2**20
        ),
        name="deconvolve",
    )(cells, ids, wts, ill_here, spread, moves, picks, observed, estimate, inv_all)


def solution(mesh):
    placed = (
        P(None, "row", "col"),
        P(None, "row", "col"),
        P(("row", "col"), None, None, None, None),
        P("row", "col", None, None),
        P("row", "col", None, None),
        P(None, "row", "col"),
    )
    return jax.shard_map(
        functools.partial(shards, mesh.shape["row"], mesh.shape["col"]),
        mesh=mesh, in_specs=placed, out_specs=P(None, "row", "col"), check_vma=False,
    )
```

time: 98.3 us -> 67.5 us (0.69)
  Pallas kernels: 90.4 us -> 63.4 us
  local copies, waits for them, and re-layouts: 6.79 us -> 4 us
    pallas_call x1, Pallas kernels: 90.4 us -> 63.4 us  [shards(): pl.pallas_call(functools.partial(kernel, n_row, n_col), out_shape=jax.Sha...]
    broadcast_in_dim x3 -> x0, local copies, waits for them, and re-layouts: 1.36 us -> none  [the longest x1 0.68 us: shards(): jnp.broadcast_to(zone_ids[0, 0].T[:, :, None], (2, depth, 128)).astype(BF)]
    unnamed x7 -> x2, local copies, waits for them, and re-layouts: 3.45 us -> 4 us
where the time goes in v1:
time: 67.5 us; the launch traced here: 67.4 us
  Pallas kernels  63.4 us (94%)
  local copies, waits for them, and re-layouts  4 us (6%)
    pallas_call x1, Pallas kernels, shards(): pl.pallas_call(functools.partial(kernel, n_row, n_col), out_shape=jax.Sha...  63.4 us
    unnamed x2, local copies, waits for them, and re-layouts  4 us

profile of v1, /device:TPU:1, one launch (start us, length us, event | category | flops | bytes accessed | tf_op | source)
XLA Modules:
  0.0 67.4 jit_solution(15048353684075731342)
XLA Ops:
  0.0 1.7 %copy.13 = f32[4,16,2,4,33]{4,1,3,0,2:T(8,128)} copy(f32[4,16,2,4,33]{4,3,2,1,0:T(4,128)} %param.12) | data formatting | bytes 135168 | tf_op args[2]
  1.7 63.4 %deconvolve.1 = f32[16,128,128]{2,1,0:T(8,128)} custom-call(f32[2,4,4,16,33]{4,3,2,1,0:T(8,128)} %bitcast.10, s32[2,16]{1,0:T(2,128)} %bitcast.12, f32[2,16]{1,0:T(2,128)} %bitcast.13, f32[16,16]{1,0:T(8,128)} %bitcast.11, bf16[128,768]{1,0:T(8,128)(2,1)} %constant.8.clone.spread, bf16[160,128]{1,0:T(8,128)(2,1)} %constant.9.clone.moves, ...), custom_call_target="tpu_custom_call" | custom-call | tf_op jit(solution)/shard_map/deconvolve/pallas_call | solution.py:417
  65.1 2.3 %copy.15 = f32[16,128,128]{2,1,0:T(8,128)} copy(f32[16,128,128]{2,1,0:T(8,128)} %deconvolve.1) | data formatting | bytes 2097152

commit v2 on v1

--- a/solution.py
+++ b/solution.py
@@ -62,10 +62,11 @@
 
 
 def kernel(
-    n_row, n_col, cells, ids_in, wts_in, ill_in, spread, moves, picks, obs_hbm, est_hbm, inv_all, out_hbm,
+    n_row, n_col, cells_hbm, ids_hbm, wts_hbm, ill_hbm, spread_hbm, moves_hbm, picks_hbm, obs_hbm, est_hbm, inv_all, out_hbm,
+    cells, ids_in, wts_in, ill_in, spread, moves, picks,
     obs, est, out, wide, bank, ids, wts, ill_here, ext0, ext1, ext2, ext3, ystrip, strips, corn, cornsend, plane, ids_z, sel_send, sel_recv, ill, inv,
     base, rt0, rt1, ctc0, ctc1, cth0, cth1, ptc, pth, cur, obs_t, rfac,
-    local_sem, est_sem, obs_sem, out_sem, psend, precv, isend, irecv, bsend, brecv, lsend, lrecv, hsend, hrecv,
+    in_sem, out_sem, psend, precv, isend, irecv, bsend, brecv, lsend, lrecv, hsend, hrecv,
 ):
     ext = (ext0, ext1, ext2, ext3)
     rt, ctc, cth = (rt0, rt1), (ctc0, ctc1), (cth0, cth1)
@@ -86,19 +87,65 @@
     up, down = lax.rem(row + n_row - 1, n_row), lax.rem(row + 1, n_row)
     left, right = lax.rem(col + n_col - 1, n_col), lax.rem(col + 1, n_col)
 
-    inv_copy = pltpu.make_async_copy(inv_all.at[row], inv, local_sem)
-    inv_copy.start()
-    est_copy = pltpu.make_async_copy(est_hbm, est, est_sem)
-    est_copy.start()
-    obs_copy = pltpu.make_async_copy(obs_hbm, obs, obs_sem)
-    obs_copy.start()
-    zones = cells.shape[1]
-    lane = lax.broadcasted_iota(jnp.int32, (depth, 128), 1)
+    barrier = pltpu.get_barrier_semaphore()
+    friends = [(row, z_col(d)) for d in range(1, planes)]
+    friends += [(row, core_col), (row, x_col)]
+    friends += [(lax.rem(row + d, n_row), col) for d in range(1, n_row)]
+    friends += [(row, left), (row, right)]
+    friends += [(up, left), (up, right), (down, left), (down, right)]
+    for friend in friends:
+        pl.semaphore_signal(barrier, inc=1, device_id=friend, device_id_type=MESH)
+
+    small = [
+        pltpu.make_async_copy(src, dst, in_sem.at[i])
+        for i, (src, dst) in enumerate([
+            (cells_hbm, cells), (ids_hbm, ids_in), (wts_hbm, wts_in), (ill_hbm, ill_in),
+            (moves_hbm, moves), (est_hbm, est), (spread_hbm, spread), (picks_hbm, picks),
+            (obs_hbm, obs), (inv_all.at[row], inv),
+        ])
+    ]
+    for c in small:
+        c.start()
+
+    has = {"u": row > 0, "d": row < n_row - 1, "l": col > 0, "r": col < n_col - 1}
+
+    def there(where):
+        ok = has[where[0]]
+        for w in where[1:]:
+            ok = jnp.logical_and(ok, has[w])
+        return ok
+
+    def zero_unless(where, refs, *at):
+        @pl.when(jnp.logical_not(there(where)))
+        def _():
+            for ref in refs:
+                part = ref.at[at]
+                part[...] = jnp.zeros(part.shape, BF)
+
+    every, low_half, high_half = slice(None), slice(0, 16), slice(16, 32)
+    zero_unless("r", ext, every, slice(128, 144), slice(0, 128))
+    zero_unless("l", ext, every, slice(144, 160), slice(0, 128))
+    zero_unless("d", [ystrip], every, every, low_half)
+    zero_unless("u", [ystrip], every, every, high_half)
+    zero_unless("dr", [corn], every, every, low_half, slice(0, 128))
+    zero_unless("ur", [corn], every, every, high_half, slice(0, 128))
+    zero_unless("dl", [corn], every, every, low_half, slice(128, 256))
+    zero_unless("ul", [corn], every, every, high_half, slice(128, 256))
+
+    for c in small[:4]:
+        c.wait()
+    zones = cells.shape[0]
+    lane = lax.broadcasted_iota(jnp.int32, (16, 128), 1)
+    quad = lax.broadcasted_iota(jnp.int32, (16, 128), 0)
     wide[...] = jnp.zeros_like(wide)
-    wide[:, :, :, :, 0:TAPS] = cells[...]
     for i in range(zones):
-        for q in range(4):
-            r, c = wide[0, i, q], wide[1, i, q]
+        for z in range(depth):
+            at = (z % GZ) * 4
+            for f in range(2):
+                wide[f, i, z // GZ, at : at + 4, 0:TAPS] = cells[i, z, f]
+    for i in range(zones):
+        for g in range(groups):
+            r, c = wide[0, i, g], wide[1, i, g]
             r_hi = r.astype(BF).astype(F32)
             total_c = jnp.sum(c, -1, keepdims=True)
             s_hi = total_c.astype(BF).astype(F32)
@@ -107,26 +154,20 @@
             packed = jnp.where(lane == 3 * TAPS, s_hi, packed)
             packed = jnp.where(lane == 3 * TAPS + 1, s_mid, packed)
             packed = jnp.where(lane == 3 * TAPS + 2, total_c - s_hi - s_mid, packed)
-            bank[i, q] = packed.astype(BF)
-    for k in range(2):
-        ids[k] = jnp.transpose(jnp.broadcast_to(ids_in[k : k + 1].astype(F32), (128, depth))).astype(BF)
-        wts[k] = jnp.transpose(jnp.broadcast_to(wts_in[k : k + 1], (128, depth)))
+            bank[i, g] = packed.astype(BF)
+    for g in range(groups):
+        for k in range(2):
+            tile_i = jnp.zeros((16, 128), F32)
+            tile_w = jnp.zeros((16, 128), F32)
+            for zz in range(GZ):
+                here = quad // 4 == zz
+                tile_i = jnp.where(here, ids_in[k, g * GZ + zz].astype(F32), tile_i)
+                tile_w = jnp.where(here, wts_in[k, g * GZ + zz], tile_w)
+            ids[g, k] = tile_i.astype(BF)
+            wts[g, k] = tile_w
     ill_here[...] = jnp.zeros_like(ill_here)
     ill_here[:, 0 : ill_in.shape[1]] = ill_in[...]
 
-    for p in range(4):
-        ext[p][:, 128:160, :] = jnp.zeros((depth, 32, 256), BF)
-    ystrip[...] = jnp.zeros_like(ystrip)
-    corn[...] = jnp.zeros_like(corn)
-
-    barrier = pltpu.get_barrier_semaphore()
-    friends = [(row, z_col(d)) for d in range(1, planes)]
-    friends += [(row, core_col), (row, x_col)]
-    friends += [(lax.rem(row + d, n_row), col) for d in range(1, n_row)]
-    friends += [(row, left), (row, right)]
-    friends += [(up, left), (up, right), (down, left), (down, right)]
-    for friend in friends:
-        pl.semaphore_signal(barrier, inc=1, device_id=friend, device_id_type=MESH)
     pl.semaphore_wait(barrier, len(friends))
 
     def remote(src, dst, s, r, to):
@@ -155,8 +196,6 @@
     ids_z[0] = ids[...]
     ill[row] = ill_here[...]
 
-    has = {"u": row > 0, "d": row < n_row - 1, "l": col > 0, "r": col < n_col - 1}
-
     def halo_copies(p, g):
         zs = pl.ds(g * GZ, GZ)
         top, bottom = pl.ds(0, 16), pl.ds(16, 16)
@@ -178,12 +217,6 @@
 
     opposite = {"u": "d", "d": "u", "l": "r", "r": "l"}
 
-    def there(where):
-        ok = has[where[0]]
-        for w in where[1:]:
-            ok = jnp.logical_and(ok, has[w])
-        return ok
-
     def halo_start(p, g):
         for where, c in halo_copies(p, g):
             @pl.when(there(where))
@@ -217,10 +250,7 @@
         cornsend[p, g] = c.astype(BF)
         halo_start(p, g)
 
-    est_copy.wait()
-
-    @pl.loop(0, groups)
-    def _(g):
+    def first_field(g):
         fields = []
         for zz in range(GZ):
             z = g * GZ + zz
@@ -229,6 +259,10 @@
             fields.append(c.astype(BF))
         pack(0, g, fields)
 
+    for c in small[4:6]:
+        c.wait()
+    pl.loop(0, groups // 2)(first_field)
+
     x_copy.wait_recv()
     forward = remote(plane.at[x_slot], plane.at[x_slot], psend.at[2], precv.at[2], (row, core_col))
     forward.start()
@@ -237,29 +271,36 @@
         c.wait_recv()
     forward.wait_recv()
 
-    def selection(d):
-        for k in range(2):
-            mine = ids_z[d, k].astype(F32)
-            picked = [jnp.zeros((depth, 128), F32) for _ in range(4)]
-            for s in range(4):
-                for i in range(4):
-                    zone = (zc * 16 + s * 4 + i).astype(F32)
-                    hit = mine == zone
-                    for q in range(4):
-                        picked[q] = jnp.where(hit, plane[s, i, q].astype(F32), picked[q])
-            for q in range(4):
-                sel_send[d, k * 4 + q] = picked[q].astype(BF)
-
-    sel_copies = [
-        remote(sel_send.at[d], sel_recv.at[d], bsend.at[d], brecv.at[d], (row, z_col(d)))
-        for d in range(1, planes)
-    ]
-    for d in range(1, planes):
-        selection(d)
-        sel_copies[d - 1].start()
-    selection(0)
-
-    inv_copy.wait()
+    def sel_copy(g, d):
+        return remote(
+            sel_send.at[g, d], sel_recv.at[g, d], bsend.at[g, d], brecv.at[g, d], (row, z_col(d))
+        )
+
+    def sel_start(g):
+        for d in range(1, planes):
+            sel_copy(g, d).start()
+
+    @pl.loop(0, groups)
+    def _(g):
+        for d in range(planes):
+            for k in range(2):
+                mine = ids_z[d, g, k].astype(F32)
+                picked = jnp.zeros((16, 128), F32)
+                for s in range(4):
+                    for i in range(4):
+                        zone = (zc * 16 + s * 4 + i).astype(F32)
+                        picked = jnp.where(mine == zone, plane[s, i, g].astype(F32), picked)
+                sel_send[g, d, k] = picked.astype(BF)
+
+        @pl.when(g == 0)
+        def _():
+            sel_start(0)
+
+    sel_start(1)
+    pl.loop(groups // 2, groups)(first_field)
+
+    for c in small[6:]:
+        c.wait()
     for c in ill_copies:
         c.wait_recv()
     coarse = ill_in.shape[1]
@@ -271,39 +312,47 @@
         )
     rfac[...] = 1.0 / fac
 
-    obs_copy.wait()
-    for c in sel_copies:
-        c.wait_recv()
-    picked = sel_send[0].astype(F32)
-    for d in range(1, planes):
-        picked = picked + sel_recv[d].astype(F32)
-    b = mm(jnp.reshape(picked, (8 * depth, 128)).astype(BF), spread[...])
-    total = jnp.zeros((depth, 128), F32)
-    for j in range(8):
-        r = b[j * depth : (j + 1) * depth]
-        total = total + wts[j // 4] * r[:, 512:640] * r[:, 640:768]
-    for j in range(8):
-        r = b[j * depth : (j + 1) * depth]
-        for t in range(4):
-            v = r[:, t * 128 : (t + 1) * 128]
-            base[t, j] = (wts[j // 4] * v) / total if t < 2 else v
+
+    def spread_taps(g):
+        for d in range(1, planes):
+            sel_copy(g, d).wait_recv()
+
+        @pl.when(g + 2 < groups)
+        def _():
+            sel_start(g + 2)
+
+        picked = sel_send[g, 0].astype(F32)
+        for d in range(1, planes):
+            picked = picked + sel_recv[g, d].astype(F32)
+        b = mm(jnp.reshape(picked, (32, 128)).astype(BF), spread[...])
+        r = (b[0:16], b[16:32])
+        total = wts[g, 0] * r[0][:, 512:640] * r[0][:, 640:768]
+        total = total + wts[g, 1] * r[1][:, 512:640] * r[1][:, 640:768]
+        for shift in (1, 2):
+            even = (quad // shift) % 2 == 0
+            total = total + jnp.where(even, pltpu.roll(total, 16 - shift, 0), pltpu.roll(total, shift, 0))
+        for k in range(2):
+            for t in range(4):
+                v = r[k][:, t * 128 : (t + 1) * 128]
+                base[t, g, k] = (wts[g, k] * v) / total if t < 2 else v
 
     low = lax.broadcasted_iota(jnp.int32, (16, 128), 1) < 64
     lower = low.astype(F32).astype(BF)
     upper = 1.0 - lower
 
-    def circulant(t, j, z):
-        b = jnp.broadcast_to(base[t, j, pl.ds(z, 1), :], (16, 128))
+    def circulant(t, j, g, zz):
+        b = jnp.broadcast_to(base[t, g, j // 4, pl.ds(zz * 4 + j % 4, 1), :], (16, 128))
         b = pltpu.roll(b, 0, 1, stride=1, stride_axis=0).astype(BF)
         return [pltpu.roll(b, 16 * i, 1) if i else b for i in range(8)]
 
-    def build(way, z):
+    def build(way, g, zz):
+        z = g * GZ + zz
         left_h = [0.0, 0.0]
         right_h = [0.0, 0.0]
         for j in range(8):
             js = slice(j * 128, (j + 1) * 128)
-            r = circulant(way, j, z)
-            c = circulant(2 + way, j, z)
+            r = circulant(way, j, g, zz)
+            c = circulant(2 + way, j, g, zz)
             for i in range(1, 7):
                 rt[way][z, i * 16 : i * 16 + 16, js] = r[i]
                 ctc[way][z, i * 16 : i * 16 + 16, js] = c[i]
@@ -354,10 +403,12 @@
     for p in range(4):
         @pl.loop(0, groups)
         def _(g):
+            if p == 0:
+                spread_taps(g)
             if p < 2:
                 @pl.loop(0, GZ)
                 def _(zz):
-                    build(p, g * GZ + zz)
+                    build(p, g, zz)
             halo_wait_recv(p, g)
             unpack(p, g)
             fields = []
@@ -388,8 +439,13 @@
     x_copy.wait_send()
     core_copy.wait_send()
     forward.wait_send()
-    for c in id_copies + ill_copies + sel_copies:
+    for c in id_copies + ill_copies:
         c.wait_send()
+    @pl.loop(0, groups)
+    def _(g):
+        for d in range(1, planes):
+            sel_copy(g, d).wait_send()
+
     for g in range(groups):
         out_copy(g).wait()
     for p in range(4):
@@ -403,7 +459,6 @@
     zones = psf_bank.shape[0]
     groups = depth // GZ
     planes = n_col // 4
-    cells = psf_bank.transpose(2, 0, 3, 1, 4)
     ids = zone_ids[0, 0].T
     wts = mix_weights[0, 0].T
     ill_here = illumination[:, :, 0]
@@ -411,33 +466,39 @@
     spread = jnp.asarray(spread_table())
     moves, picks = map(jnp.asarray, moves_table())
     inv_all = jnp.asarray(smoothing_table(length, n_row, rows))
-    vmem = pl.BlockSpec(memory_space=pltpu.VMEM)
     hbm = pl.BlockSpec(memory_space=pl.ANY)
     dma = pltpu.SemaphoreType.DMA
     return pl.pallas_call(
         functools.partial(kernel, n_row, n_col),
         out_shape=jax.ShapeDtypeStruct(estimate.shape, F32),
-        in_specs=[vmem] * 7 + [hbm] * 3,
-        out_specs=hbm,
+        in_specs=[hbm] * 10,
+        out_specs=pl.BlockSpec(memory_space=pl.ANY),
         scratch_shapes=[
+            pltpu.VMEM(psf_bank.shape, F32),
+            pltpu.SMEM(ids.shape, jnp.int32),
+            pltpu.SMEM(wts.shape, F32),
+            pltpu.VMEM(ill_here.shape, F32),
+            pltpu.VMEM(spread.shape, BF),
+            pltpu.VMEM(moves.shape, BF),
+            pltpu.VMEM(picks.shape, BF),
             *[pltpu.VMEM((depth, rows, cols), F32)] * 3,
-            pltpu.VMEM((2, zones, 4, depth, 128), F32),
-            pltpu.VMEM((zones, 4, depth, 128), BF),
-            pltpu.VMEM((2, depth, 128), BF),
-            pltpu.VMEM((2, depth, 128), F32),
+            pltpu.VMEM((2, zones, groups, 16, 128), F32),
+            pltpu.VMEM((zones, groups, 16, 128), BF),
+            pltpu.VMEM((groups, 2, 16, 128), BF),
+            pltpu.VMEM((groups, 2, 16, 128), F32),
             pltpu.VMEM((depth, 128), F32),
             *[pltpu.VMEM((depth, 160, 256), BF)] * 4,
             pltpu.VMEM((4, depth, 32, 128), BF),
             pltpu.VMEM((4, depth, 32, 128), BF),
             pltpu.VMEM((4, groups, 32, 256), BF),
             pltpu.VMEM((4, groups, 32, 128), BF),
-            pltpu.VMEM((4, zones, 4, depth, 128), BF),
-            pltpu.VMEM((planes, 2, depth, 128), BF),
-            pltpu.VMEM((planes, 8, depth, 128), BF),
-            pltpu.VMEM((planes, 8, depth, 128), BF),
+            pltpu.VMEM((4, zones, groups, 16, 128), BF),
+            pltpu.VMEM((planes, groups, 2, 16, 128), BF),
+            pltpu.VMEM((groups, planes, 2, 16, 128), BF),
+            pltpu.VMEM((groups, planes, 2, 16, 128), BF),
             pltpu.VMEM((n_row, depth, 128), F32),
             pltpu.VMEM((length, rows), F32),
-            pltpu.VMEM((4, 8, depth, 128), F32),
+            pltpu.VMEM((4, groups, 2, 16, 128), F32),
             *[pltpu.VMEM((depth, 160, 1024), BF)] * 2,
             *[pltpu.VMEM((depth, 128, 1024), BF)] * 2,
             *[pltpu.VMEM((depth, 128, 256), BF)] * 2,
@@ -446,10 +507,10 @@
             pltpu.VMEM((depth, 128, 128), F32),
             pltpu.VMEM((depth, 128, 128), F32),
             pltpu.VMEM((depth, 128), F32),
-            dma, dma, dma, dma((groups,)),
+            dma((10,)), dma((groups,)),
             dma((3,)), dma((3,)),
             dma((planes,)), dma((planes,)),
-            dma((planes,)), dma((planes,)),
+            dma((groups, planes)), dma((groups, planes)),
             dma((n_row,)), dma((n_row,)),
             dma((4, groups, 8)), dma((4, groups, 8)),
         ],
@@ -457,7 +518,7 @@
             collective_id=0, has_side_effects=True, vmem_limit_bytes=60 * 2**20
         ),
         name="deconvolve",
-    )(cells, ids, wts, ill_here, spread, moves, picks, observed, estimate, inv_all)
+    )(psf_bank, ids, wts, ill_here, spread, moves, picks, observed, estimate, inv_all)
 
 
 def solution(mesh):

time: 67.5 us -> 64.3 us (0.953)
  local copies, waits for them, and re-layouts: 4 us -> 2.3 us
  Pallas kernels: 63.4 us -> 61.9 us
    unnamed x2 -> x1, local copies, waits for them, and re-layouts: 4 us -> 2.3 us
    pallas_call x1, Pallas kernels: 63.4 us -> 61.9 us  [shards(): pl.pallas_call(functools.partial(kernel, n_row, n_col), out_shape=jax.Sha...]
where the time goes in v2:
time: 64.3 us; the launch traced here: 64.2 us
  Pallas kernels  61.9 us (96%)
  local copies, waits for them, and re-layouts  2.3 us (4%)
    pallas_call x1, Pallas kernels, shards(): pl.pallas_call(functools.partial(kernel, n_row, n_col), out_shape=jax.Sha...  61.9 us
    unnamed x1, local copies, waits for them, and re-layouts  2.3 us

profile of v2, /device:TPU:1, one launch (start us, length us, event | category | flops | bytes accessed | tf_op | source)
XLA Modules:
  0.0 64.2 jit_solution(5338132885494981743)
XLA Ops:
  0.0 61.9 %deconvolve.1 = f32[16,128,128]{2,1,0:T(8,128)} custom-call(f32[4,16,2,4,33]{4,3,2,1,0:T(4,128)} %cells_hbm.1, s32[2,16]{1,0:T(2,128)} %bitcast.8, f32[2,16]{1,0:T(2,128)} %bitcast.9, f32[16,16]{1,0:T(8,128)} %bitcast.7, bf16[128,768]{1,0:T(8,128)(2,1)} %constant.8.clone.spread_hbm, bf16[160,128]{1,0:T(8,128)(2,1)} %constant.9.clone.moves_hbm, ...), custom_call_target="tpu_custom_call" | custom-call | tf_op jit(solution)/shard_map/deconvolve/pallas_call | solution.py:471
  61.9 2.3 %copy.12 = f32[16,128,128]{2,1,0:T(8,128)} copy(f32[16,128,128]{2,1,0:T(8,128)} %deconvolve.1) | data formatting | bytes 2097152

commit v3 on v2

--- a/solution.py
+++ b/solution.py
@@ -65,11 +65,11 @@
     n_row, n_col, cells_hbm, ids_hbm, wts_hbm, ill_hbm, spread_hbm, moves_hbm, picks_hbm, obs_hbm, est_hbm, inv_all, out_hbm,
     cells, ids_in, wts_in, ill_in, spread, moves, picks,
     obs, est, out, wide, bank, ids, wts, ill_here, ext0, ext1, ext2, ext3, ystrip, strips, corn, cornsend, plane, ids_z, sel_send, sel_recv, ill, inv,
-    base, rt0, rt1, ctc0, ctc1, cth0, cth1, ptc, pth, cur, obs_t, rfac,
+    base, rt0, rt1, ctc0, ctc1, ptc, cur, obs_t, rfac,
     in_sem, out_sem, psend, precv, isend, irecv, bsend, brecv, lsend, lrecv, hsend, hrecv,
 ):
     ext = (ext0, ext1, ext2, ext3)
-    rt, ctc, cth = (rt0, rt1), (ctc0, ctc1), (cth0, cth1)
+    rt, ctc = (rt0, rt1), (ctc0, ctc1)
     depth = obs.shape[0]
     groups = depth // GZ
     planes = n_col // 4
@@ -366,10 +366,10 @@
             left_h[j // 4] += pltpu.roll(c[0] * upper, (at + 16 + 16) % 128, 1)
             right_h[j // 4] += pltpu.roll(c[7] * lower, at, 1) if at else c[7] * lower
         for h in range(2):
-            hs = slice(h * 128, (h + 1) * 128)
-            cth[way][z, 0:16, hs] = left_h[h]
-            cth[way][z, 16:112, hs] = jnp.zeros((96, 128), BF)
-            cth[way][z, 112:128, hs] = right_h[h]
+            hs = slice(1024 + h * 128, 1152 + h * 128)
+            ctc[way][z, 0:16, hs] = left_h[h]
+            ctc[way][z, 16:112, hs] = jnp.zeros((96, 128), BF)
+            ctc[way][z, 112:128, hs] = right_h[h]
 
     def out_copy(g):
         zs = pl.ds(g * GZ, GZ)
@@ -395,10 +395,10 @@
             for h in range(2):
                 j = jp * 2 + h
                 ptc[zz, j * 128 : (j + 1) * 128] = o[0:128, h * 128 : (h + 1) * 128]
-                pth[zz, j * 32 : (j + 1) * 32] = o[128:160, h * 128 : (h + 1) * 128]
+                ptc[zz, 1024 + j * 32 : 1056 + j * 32] = o[128:160, h * 128 : (h + 1) * 128]
 
     def cols_stage(p, z, zz):
-        return mm(ctc[p % 2][z], ptc[zz]) + mm(cth[p % 2][z], pth[zz])
+        return mm(ctc[p % 2][z], ptc[zz])
 
     for p in range(4):
         @pl.loop(0, groups)
@@ -500,10 +500,8 @@
             pltpu.VMEM((length, rows), F32),
             pltpu.VMEM((4, groups, 2, 16, 128), F32),
             *[pltpu.VMEM((depth, 160, 1024), BF)] * 2,
-            *[pltpu.VMEM((depth, 128, 1024), BF)] * 2,
-            *[pltpu.VMEM((depth, 128, 256), BF)] * 2,
-            pltpu.VMEM((GZ, 1024, 128), BF),
-            pltpu.VMEM((GZ, 256, 128), BF),
+            *[pltpu.VMEM((depth, 128, 1280), BF)] * 2,
+            pltpu.VMEM((GZ, 1280, 128), BF),
             pltpu.VMEM((depth, 128, 128), F32),
             pltpu.VMEM((depth, 128, 128), F32),
             pltpu.VMEM((depth, 128), F32),
@@ -515,10 +513,10 @@
             dma((4, groups, 8)), dma((4, groups, 8)),
         ],
         compiler_params=pltpu.CompilerParams(
-            collective_id=0, has_side_effects=True, vmem_limit_bytes=60 * 2**20
+            collective_id=0, has_side_effects=True, vmem_limit_bytes=44 * 2**20
         ),
         name="deconvolve",
-    )(psf_bank, ids, wts, ill_here, spread, moves, picks, observed, estimate, inv_all)
+    )(*[pltpu.with_memory_space_constraint(v, pltpu.HBM) for v in (psf_bank, ids, wts, ill_here, spread, moves, picks, observed, estimate, inv_all)])
 
 
 def solution(mesh):

time: 64.3 us -> 61.2 us (0.952)
  Pallas kernels: 61.9 us -> 60.1 us
  local copies, waits for them, and re-layouts: 2.3 us -> 0.97 us
    pallas_call x1, Pallas kernels: 61.9 us -> 60.1 us  [shards(): pl.pallas_call(functools.partial(kernel, n_row, n_col), out_shape=jax.Sha...]
    unnamed x1, local copies, waits for them, and re-layouts: 2.3 us -> 0.97 us
where the time goes in v3:
time: 61.2 us; the launch traced here: 61.1 us
  Pallas kernels  60.1 us (98%)
  local copies, waits for them, and re-layouts  0.97 us (2%)
    pallas_call x1, Pallas kernels, shards(): pl.pallas_call(functools.partial(kernel, n_row, n_col), out_shape=jax.Sha...  60.1 us

profile of v3, /device:TPU:1, one launch (start us, length us, event | category | flops | bytes accessed | tf_op | source)
XLA Modules:
  0.0 61.1 jit_solution(8970373592435294352)
XLA Ops:
  0.0 60.1 %deconvolve.1 = f32[16,128,128]{2,1,0:T(8,128)S(1)} custom-call(f32[4,16,2,4,33]{4,3,2,1,0:T(4,128)} %cells_hbm.1, s32[2,16]{1,0:T(2,128)} %bitcast.8, f32[2,16]{1,0:T(2,128)} %bitcast.9, f32[16,16]{1,0:T(8,128)} %bitcast.7, bf16[128,768]{1,0:T(8,128)(2,1)} %constant.8.clone.spread_hbm, bf16[160,128]{1,0:T(8,128)(2,1)} %constant.9.clone.moves_hbm, ...), custom_call_target="tpu_custom_call" | custom-call | tf_op jit(solution)/shard_map/deconvolve/pallas_call | solution.py:471
  60.1 1.0 %copy.12 = f32[16,128,128]{2,1,0:T(8,128)} copy(f32[16,128,128]{2,1,0:T(8,128)S(1)} %deconvolve.1) | data formatting | bytes 2097152

commit v4 on v3

--- a/solution.py
+++ b/solution.py
@@ -78,8 +78,7 @@
     zc = col // 4
     slot = lax.rem(col, 4)
     core_col = zc * 4 + slot + 1 - 2 * lax.rem(slot, 2)
-    x_slot = lax.rem(slot + 2, 4)
-    x_col = zc * 4 + x_slot
+    x_col = zc * 4 + lax.rem(slot + 2, 4)
 
     def z_col(d):
         return lax.rem(zc + d + planes, planes) * 4 + slot
@@ -89,7 +88,7 @@
 
     barrier = pltpu.get_barrier_semaphore()
     friends = [(row, z_col(d)) for d in range(1, planes)]
-    friends += [(row, core_col), (row, x_col)]
+    friends += [(row, core_col), (row, x_col), (row, zc * 4 + 3 - slot)]
     friends += [(lax.rem(row + d, n_row), col) for d in range(1, n_row)]
     friends += [(row, left), (row, right)]
     friends += [(up, left), (up, right), (down, left), (down, right)]
@@ -154,17 +153,19 @@
             packed = jnp.where(lane == 3 * TAPS, s_hi, packed)
             packed = jnp.where(lane == 3 * TAPS + 1, s_mid, packed)
             packed = jnp.where(lane == 3 * TAPS + 2, total_c - s_hi - s_mid, packed)
-            bank[i, g] = packed.astype(BF)
+            bank[g, i] = packed.astype(BF)
+    tile_i = jnp.zeros((16, 128), F32)
     for g in range(groups):
         for k in range(2):
-            tile_i = jnp.zeros((16, 128), F32)
+            lanes_here = lane // 16 == g * 2 + k
             tile_w = jnp.zeros((16, 128), F32)
             for zz in range(GZ):
                 here = quad // 4 == zz
-                tile_i = jnp.where(here, ids_in[k, g * GZ + zz].astype(F32), tile_i)
+                both = jnp.logical_and(here, lanes_here)
+                tile_i = jnp.where(both, ids_in[k, g * GZ + zz].astype(F32), tile_i)
                 tile_w = jnp.where(here, wts_in[k, g * GZ + zz], tile_w)
-            ids[g, k] = tile_i.astype(BF)
             wts[g, k] = tile_w
+    ids[...] = tile_i.astype(BF)
     ill_here[...] = jnp.zeros_like(ill_here)
     ill_here[:, 0 : ill_in.shape[1]] = ill_in[...]
 
@@ -175,10 +176,19 @@
             src_ref=src, dst_ref=dst, send_sem=s, recv_sem=r, device_id=to, device_id_type=MESH
         )
 
-    x_copy = remote(bank, plane.at[slot], psend.at[0], precv.at[0], (row, x_col))
-    core_copy = remote(bank, plane.at[slot], psend.at[1], precv.at[1], (row, core_col))
-    x_copy.start()
-    core_copy.start()
+    far_col = zc * 4 + 3 - slot
+
+    def plane_copies(g):
+        return [
+            remote(bank.at[g], plane.at[g, slot], psend.at[g, i], precv.at[g, i], (row, to))
+            for i, to in enumerate((x_col, far_col, core_col))
+        ]
+
+    def plane_start(g):
+        for c in plane_copies(g):
+            c.start()
+
+    plane_start(0)
     id_copies = [
         remote(ids, ids_z.at[d], isend.at[d], irecv.at[d], (row, z_col(-d))) for d in range(1, planes)
     ]
@@ -190,9 +200,8 @@
         )
         for d in range(1, n_row)
     ]
-    for c in ill_copies:
-        c.start()
-    plane[slot] = bank[...]
+    for g in range(groups):
+        plane[g, slot] = bank[g]
     ids_z[0] = ids[...]
     ill[row] = ill_here[...]
 
@@ -261,57 +270,53 @@
 
     for c in small[4:6]:
         c.wait()
-    pl.loop(0, groups // 2)(first_field)
-
-    x_copy.wait_recv()
-    forward = remote(plane.at[x_slot], plane.at[x_slot], psend.at[2], precv.at[2], (row, core_col))
-    forward.start()
-    core_copy.wait_recv()
+    for g in range(groups):
+        if g:
+            plane_start(g)
+        first_field(g)
+    for c in ill_copies:
+        c.start()
+
     for c in id_copies:
         c.wait_recv()
-    forward.wait_recv()
 
     def sel_copy(g, d):
         return remote(
             sel_send.at[g, d], sel_recv.at[g, d], bsend.at[g, d], brecv.at[g, d], (row, z_col(d))
         )
 
-    def sel_start(g):
-        for d in range(1, planes):
-            sel_copy(g, d).start()
-
-    @pl.loop(0, groups)
-    def _(g):
+    def select(g):
+        for c in plane_copies(g):
+            c.wait_recv()
         for d in range(planes):
             for k in range(2):
-                mine = ids_z[d, g, k].astype(F32)
+                one = jnp.where(lane == (g * 2 + k) * 16, ids_z[d].astype(F32), 0.0)
+                mine = jnp.broadcast_to(jnp.sum(one, -1, keepdims=True), (16, 128))
                 picked = jnp.zeros((16, 128), F32)
                 for s in range(4):
                     for i in range(4):
                         zone = (zc * 16 + s * 4 + i).astype(F32)
-                        picked = jnp.where(mine == zone, plane[s, i, g].astype(F32), picked)
+                        picked = jnp.where(mine == zone, plane[g, s, i].astype(F32), picked)
                 sel_send[g, d, k] = picked.astype(BF)
-
-        @pl.when(g == 0)
-        def _():
-            sel_start(0)
-
-    sel_start(1)
-    pl.loop(groups // 2, groups)(first_field)
+        for d in range(1, planes):
+            sel_copy(g, d).start()
+
+    pl.loop(0, 2)(select)
 
     for c in small[6:]:
         c.wait()
-    for c in ill_copies:
-        c.wait_recv()
-    coarse = ill_in.shape[1]
-    fac = jnp.zeros((depth, inv.shape[1]), F32)
-    for i in range(n_row):
-        fac = fac + jnp.dot(
-            ill[i, :, 0:coarse], inv[i * coarse : (i + 1) * coarse],
-            precision=lax.Precision.HIGHEST, preferred_element_type=F32,
-        )
-    rfac[...] = 1.0 / fac
-
+
+    def smooth():
+        for c in ill_copies:
+            c.wait_recv()
+        coarse = ill_in.shape[1]
+        fac = jnp.zeros((depth, inv.shape[1]), F32)
+        for i in range(n_row):
+            fac = fac + jnp.dot(
+                ill[i, :, 0:coarse], inv[i * coarse : (i + 1) * coarse],
+                precision=lax.Precision.HIGHEST, preferred_element_type=F32,
+            )
+        rfac[...] = 1.0 / fac
 
     def spread_taps(g):
         for d in range(1, planes):
@@ -319,7 +324,7 @@
 
         @pl.when(g + 2 < groups)
         def _():
-            sel_start(g + 2)
+            select(g + 2)
 
         picked = sel_send[g, 0].astype(F32)
         for d in range(1, planes):
@@ -401,6 +406,9 @@
         return mm(ctc[p % 2][z], ptc[zz])
 
     for p in range(4):
+        if p == 1:
+            smooth()
+
         @pl.loop(0, groups)
         def _(g):
             if p == 0:
@@ -436,9 +444,9 @@
             else:
                 out_copy(g).start()
 
-    x_copy.wait_send()
-    core_copy.wait_send()
-    forward.wait_send()
+    for g in range(groups):
+        for c in plane_copies(g):
+            c.wait_send()
     for c in id_copies + ill_copies:
         c.wait_send()
     @pl.loop(0, groups)
@@ -483,8 +491,8 @@
             pltpu.VMEM(picks.shape, BF),
             *[pltpu.VMEM((depth, rows, cols), F32)] * 3,
             pltpu.VMEM((2, zones, groups, 16, 128), F32),
-            pltpu.VMEM((zones, groups, 16, 128), BF),
-            pltpu.VMEM((groups, 2, 16, 128), BF),
+            pltpu.VMEM((groups, zones, 16, 128), BF),
+            pltpu.VMEM((16, 128), BF),
             pltpu.VMEM((groups, 2, 16, 128), F32),
             pltpu.VMEM((depth, 128), F32),
             *[pltpu.VMEM((depth, 160, 256), BF)] * 4,
@@ -492,8 +500,8 @@
             pltpu.VMEM((4, depth, 32, 128), BF),
             pltpu.VMEM((4, groups, 32, 256), BF),
             pltpu.VMEM((4, groups, 32, 128), BF),
-            pltpu.VMEM((4, zones, groups, 16, 128), BF),
-            pltpu.VMEM((planes, groups, 2, 16, 128), BF),
+            pltpu.VMEM((groups, 4, zones, 16, 128), BF),
+            pltpu.VMEM((planes, 16, 128), BF),
             pltpu.VMEM((groups, planes, 2, 16, 128), BF),
             pltpu.VMEM((groups, planes, 2, 16, 128), BF),
             pltpu.VMEM((n_row, depth, 128), F32),
@@ -506,7 +514,7 @@
             pltpu.VMEM((depth, 128, 128), F32),
             pltpu.VMEM((depth, 128), F32),
             dma((10,)), dma((groups,)),
-            dma((3,)), dma((3,)),
+            dma((groups, 3)), dma((groups, 3)),
             dma((planes,)), dma((planes,)),
             dma((groups, planes)), dma((groups, planes)),
             dma((n_row,)), dma((n_row,)),

time: 61.2 us -> 57.8 us (0.944)
  Pallas kernels: 60.1 us -> 56.7 us
    pallas_call x1, Pallas kernels: 60.1 us -> 56.7 us  [shards(): pl.pallas_call(functools.partial(kernel, n_row, n_col), out_shape=jax.Sha...]
where the time goes in v4:
time: 57.8 us; the launch traced here: 57.7 us
  Pallas kernels  56.7 us (98%)
  local copies, waits for them, and re-layouts  0.97 us (2%)
    pallas_call x1, Pallas kernels, shards(): pl.pallas_call(functools.partial(kernel, n_row, n_col), out_shape=jax.Sha...  56.7 us

profile of v4, /device:TPU:1, one launch (start us, length us, event | category | flops | bytes accessed | tf_op | source)
XLA Modules:
  0.0 57.7 jit_solution(2141048445322683360)
XLA Ops:
  0.0 56.7 %deconvolve.1 = f32[16,128,128]{2,1,0:T(8,128)S(1)} custom-call(f32[4,16,2,4,33]{4,3,2,1,0:T(4,128)} %cells_hbm.1, s32[2,16]{1,0:T(2,128)} %bitcast.8, f32[2,16]{1,0:T(2,128)} %bitcast.9, f32[16,16]{1,0:T(8,128)} %bitcast.7, bf16[128,768]{1,0:T(8,128)(2,1)} %constant.8.clone.spread_hbm, bf16[160,128]{1,0:T(8,128)(2,1)} %constant.9.clone.moves_hbm, ...), custom_call_target="tpu_custom_call" | custom-call | tf_op jit(solution)/shard_map/deconvolve/pallas_call | solution.py:479
  56.7 1.0 %copy.12 = f32[16,128,128]{2,1,0:T(8,128)} copy(f32[16,128,128]{2,1,0:T(8,128)S(1)} %deconvolve.1) | data formatting | bytes 2097152

commit v5 on v4

--- a/solution.py
+++ b/solution.py
@@ -301,7 +301,7 @@
         for d in range(1, planes):
             sel_copy(g, d).start()
 
-    pl.loop(0, 2)(select)
+    pl.loop(0, 4)(select)
 
     for c in small[6:]:
         c.wait()
@@ -321,10 +321,6 @@
     def spread_taps(g):
         for d in range(1, planes):
             sel_copy(g, d).wait_recv()
-
-        @pl.when(g + 2 < groups)
-        def _():
-            select(g + 2)
 
         picked = sel_send[g, 0].astype(F32)
         for d in range(1, planes):

time: 57.8 us -> 57.3 us (level)
  no operation moved by 1% of the time
where the time goes in v5:
time: 57.3 us; the launch traced here: 57.2 us
  Pallas kernels  56.3 us (98%)
  local copies, waits for them, and re-layouts  0.97 us (2%)
    pallas_call x1, Pallas kernels, shards(): pl.pallas_call(functools.partial(kernel, n_row, n_col), out_shape=jax.Sha...  56.3 us

profile of v5, /device:TPU:1, one launch (start us, length us, event | category | flops | bytes accessed | tf_op | source)
XLA Modules:
  0.0 57.2 jit_solution(7866587561169811157)
XLA Ops:
  0.0 56.3 %deconvolve.1 = f32[16,128,128]{2,1,0:T(8,128)S(1)} custom-call(f32[4,16,2,4,33]{4,3,2,1,0:T(4,128)} %cells_hbm.1, s32[2,16]{1,0:T(2,128)} %bitcast.8, f32[2,16]{1,0:T(2,128)} %bitcast.9, f32[16,16]{1,0:T(8,128)} %bitcast.7, bf16[128,768]{1,0:T(8,128)(2,1)} %constant.8.clone.spread_hbm, bf16[160,128]{1,0:T(8,128)(2,1)} %constant.9.clone.moves_hbm, ...), custom_call_target="tpu_custom_call" | custom-call | tf_op jit(solution)/shard_map/deconvolve/pallas_call | solution.py:475
  56.3 1.0 %copy.12 = f32[16,128,128]{2,1,0:T(8,128)} copy(f32[16,128,128]{2,1,0:T(8,128)S(1)} %deconvolve.1) | data formatting | bytes 2097152
